TPU v7x, 32 devices: a whole 2x2x4 slice. The times are simulated.
32 devices in a mesh: dp: 4 (over x, core), ctx: 4 (over z), fsdp: 2 (over y).
Axes of the slice: x: 2, y: 2, z: 4, core: 2. Of those that a mesh axis runs over, the one named last changes fastest.
Arguments:
- tokens: bfloat16 [16, 2048, 768], P(('dp', 'fsdp'), 'ctx'), may hold values from -6 to 6
- cotangent: bfloat16 [16, 2048, 768], P(('dp', 'fsdp'), 'ctx'), may hold values from -6 to 6
- qkv_weight: bfloat16 [768, 2304], P(('dp', 'fsdp')), may hold values from -8 to 8
- out_weight: bfloat16 [768, 768], P(('dp', 'fsdp')), may hold values from -0.75 to 0.75
- up_weight: bfloat16 [768, 2304], P(('dp', 'fsdp')), may hold values from -0.21875 to 0.21875
- down_weight: bfloat16 [1152, 768], P(('dp', 'fsdp')), may hold values from -0.1875 to 0.1875
- attention_gain: bfloat16 [768], P(('dp', 'fsdp')), may hold values from 0.25 to 1.75
- feedforward_gain: bfloat16 [768], P(('dp', 'fsdp')), may hold values from 0.25 to 1.75
Outputs:
- output: bfloat16 [16, 2048, 768], P(('dp', 'fsdp'), 'ctx')
- token_grad: float32 [16, 2048, 768], P(('dp', 'fsdp'), 'ctx')
- grad_qkv: float32 [768, 2304], P(('dp', 'fsdp'))
- grad_out: float32 [768, 768], P(('dp', 'fsdp'))
- grad_up: float32 [768, 2304], P(('dp', 'fsdp'))
- grad_down: float32 [1152, 768], P(('dp', 'fsdp'))
- grad_attention_gain: float32 [768], P(('dp', 'fsdp'))
- grad_feedforward_gain: float32 [768], P(('dp', 'fsdp'))
All inputs are finite; a program needn't handle non-finite values.
Results may differ from a plain program's by a relative error of at most 0.02.
Values may be sent and summed in bfloat16 or wider, within the bound.
A program may use at most 320 MiB of HBM per device.

v0:
```python
from functools import partial

import jax
import jax.numpy as jnp
from jax import lax
from jax.sharding import PartitionSpec as P

D = 768
HEADS = 12
HEAD = 64
FF = 1152


norm_eps = 1e-05
rope_base = 160000.0
block_rows = 512


def layer_norm(values, norm_gain):
    centre = jnp.mean(values, -1, keepdims=True)
    centred = values - centre
    inverse = lax.rsqrt(jnp.mean(centred * centred, -1, keepdims=True) + norm_eps)
    normed = centred * inverse
    return (normed, inverse, normed * norm_gain)


def norm_back(upstream, normed, inverse, norm_gain):
    scaled = upstream * norm_gain
    return (
        scaled
        - jnp.mean(scaled, -1, keepdims=True)
        - normed * jnp.mean(scaled * normed, -1, keepdims=True)
    ) * inverse


def gated_gelu(inputs, gating):
    return jax.nn.gelu(inputs, approximate=False) * gating


def rope_tables(positions, head_size):
    half_size = head_size // 2
    frequency = rope_base ** (-2.0 * jnp.arange(half_size, dtype=jnp.float32) / head_size)
    angles = positions.astype(jnp.float32)[:, None] * frequency[None, :]
    cosine = jnp.cos(angles)
    sine_half = jnp.sin(angles)
    return (jnp.concatenate([cosine, cosine], -1), jnp.concatenate([sine_half, sine_half], -1))


def rotate_heads(values, cosine_table, sine_table):
    half_size = values.shape[-1] // 2
    turned = jnp.concatenate([-values[..., half_size:], values[..., :half_size]], -1)
    return values * cosine_table[:, None, :] + turned * sine_table[:, None, :]


def outer_sum(left_rows, right_rows):
    return lax.dot_general(
        left_rows, right_rows, (((0,), (0,)), ((), ())), preferred_element_type=jnp.float32
    )


def in_blocks(step_fn, state_now, key_piece, first_row):
    length = key_piece.shape[2]

    def inner_step(number, current):
        offset = number * block_rows
        sub_piece = lax.dynamic_slice_in_dim(key_piece, offset, block_rows, 2)
        return step_fn(current, sub_piece, offset)

    return lax.fori_loop(0, length // block_rows, inner_step, state_now)


def split_heads(key_block):
    flat_shape = (key_block.shape[1], key_block.shape[2], HEADS, HEAD)
    return (key_block[0].reshape(flat_shape), key_block[1].reshape(flat_shape))


def softmax_block(state_now, key_block, first_row, query_heads, score_scale):
    highest, denominator, weighted = state_now
    key_heads, value_heads = split_heads(key_block)
    scores = (
        jnp.einsum("sbhd,srhd->shbr", query_heads, key_heads, preferred_element_type=jnp.float32)
        * score_scale
    )
    new_high = jnp.maximum(highest, jnp.max(scores, -1))
    factor = jnp.exp(highest - new_high)
    weights = jnp.exp(scores - new_high[..., None])
    denominator = denominator * factor + jnp.sum(weights, -1)
    weighted = weighted * factor[..., None] + jnp.einsum(
        "shbr,srhd->shbd",
        weights.astype(jnp.bfloat16),
        value_heads,
        preferred_element_type=jnp.float32,
    )
    return (new_high, denominator, weighted)


def gradient_step(
    state_now, key_block, first_row, query_heads, upstream_heads, log_total, delta_sum, score_scale
):
    query_acc, key_acc = state_now
    key_heads, value_heads = split_heads(key_block)
    scores = (
        jnp.einsum("sbhd,srhd->shbr", query_heads, key_heads, preferred_element_type=jnp.float32)
        * score_scale
    )
    weights = jnp.exp(scores - log_total[..., None])
    weight_grad = jnp.einsum(
        "sbhd,srhd->shbr", upstream_heads, value_heads, preferred_element_type=jnp.float32
    )
    score_grad = (weights * (weight_grad - delta_sum[..., None])).astype(jnp.bfloat16)
    query_term = (
        jnp.einsum("shbr,srhd->sbhd", score_grad, key_heads, preferred_element_type=jnp.float32)
        * score_scale
    )
    key_term = (
        jnp.einsum("shbr,sbhd->srhd", score_grad, query_heads, preferred_element_type=jnp.float32)
        * score_scale
    )
    value_term = jnp.einsum(
        "shbr,sbhd->srhd",
        weights.astype(jnp.bfloat16),
        upstream_heads,
        preferred_element_type=jnp.float32,
    )
    flat_shape = (key_block.shape[1], key_block.shape[2], key_block.shape[3])
    both_terms = jnp.stack([key_term.reshape(flat_shape), value_term.reshape(flat_shape)])
    earlier = lax.dynamic_slice_in_dim(key_acc, first_row, key_block.shape[2], 2)
    return (
        query_acc + query_term,
        lax.dynamic_update_slice_in_dim(key_acc, earlier + both_terms, first_row, 2),
    )


def body(
    tokens,
    cotangent,
    qkv_weight,
    out_weight,
    up_weight,
    down_weight,
    attention_gain,
    feedforward_gain,
):
    qkv_whole, out_whole, up_whole, down_whole, attn_gain_whole, ffn_gain_whole = (
        lax.all_gather(qkv_weight, ("dp", "fsdp"), axis=0, tiled=True),
        lax.all_gather(out_weight, ("dp", "fsdp"), axis=0, tiled=True),
        lax.all_gather(up_weight, ("dp", "fsdp"), axis=0, tiled=True),
        lax.all_gather(down_weight, ("dp", "fsdp"), axis=0, tiled=True),
        lax.all_gather(attention_gain, ("dp", "fsdp"), axis=0, tiled=True),
        lax.all_gather(feedforward_gain, ("dp", "fsdp"), axis=0, tiled=True),
    )
    attn_gain = attn_gain_whole.astype(jnp.float32)
    ffn_gain = ffn_gain_whole.astype(jnp.float32)
    seq_count, block_len = (tokens.shape[0], tokens.shape[1])
    row_count = seq_count * block_len
    score_scale = HEAD ** (-0.5)
    inputs = tokens.reshape(row_count, D).astype(jnp.float32)
    normed_a, inverse_a, scaled_a = layer_norm(inputs, attn_gain)
    normal_a = scaled_a.astype(jnp.bfloat16)
    projected = jnp.dot(normal_a, qkv_whole, preferred_element_type=jnp.float32)
    positions = lax.axis_index("ctx") * block_len + jnp.arange(block_len, dtype=jnp.int32)
    cosine_table, sine_table = rope_tables(positions, HEAD)
    head_shape = (seq_count, block_len, HEADS, HEAD)
    query_heads = rotate_heads(
        projected[:, :D].reshape(head_shape), cosine_table, sine_table
    ).astype(jnp.bfloat16)
    key_heads = rotate_heads(
        projected[:, D : 2 * D].reshape(head_shape), cosine_table, sine_table
    ).astype(jnp.bfloat16)
    value_flat = projected[:, 2 * D :].astype(jnp.bfloat16)
    key_value = jnp.stack(
        [key_heads.reshape(seq_count, block_len, D), value_flat.reshape(seq_count, block_len, D)]
    )
    stat_shape = (seq_count, HEADS, block_len)
    start_state = (
        jnp.full(stat_shape, -1e30, jnp.float32),
        jnp.zeros(stat_shape, jnp.float32),
        jnp.zeros((seq_count, HEADS, block_len, HEAD), jnp.float32),
    )
    forward_fold = partial(
        in_blocks, partial(softmax_block, query_heads=query_heads, score_scale=score_scale)
    )
    highest, denominator, weighted = forward_fold(
        start_state, lax.all_gather(key_value, "ctx", axis=2, tiled=True), jnp.int32(0)
    )
    log_total = highest + jnp.log(denominator)
    attended = jnp.transpose(weighted / denominator[..., None], (0, 2, 1, 3)).astype(jnp.bfloat16)
    attended_flat = attended.reshape(row_count, D)
    residual = inputs + jnp.dot(attended_flat, out_whole, preferred_element_type=jnp.float32)
    normed_b, inverse_b, scaled_b = layer_norm(residual, ffn_gain)
    normal_b = scaled_b.astype(jnp.bfloat16)
    widened = jnp.dot(normal_b, up_whole, preferred_element_type=jnp.float32)
    hidden, hidden_back = jax.vjp(gated_gelu, widened[:, :FF], widened[:, FF:])
    hidden_low = hidden.astype(jnp.bfloat16)
    output = (
        residual + jnp.dot(hidden_low, down_whole, preferred_element_type=jnp.float32)
    ).astype(jnp.bfloat16)
    cotangent_rows = cotangent.reshape(row_count, D)
    down_grad = outer_sum(hidden_low, cotangent_rows)
    hidden_grad = jnp.dot(cotangent_rows, down_whole.T, preferred_element_type=jnp.float32)
    input_grad, gating_grad = hidden_back(hidden_grad)
    widened_grad = jnp.concatenate([input_grad, gating_grad], -1).astype(jnp.bfloat16)
    up_grad = outer_sum(normal_b, widened_grad)
    normal_b_grad = jnp.dot(widened_grad, up_whole.T, preferred_element_type=jnp.float32)
    ffn_gain_grad = jnp.sum(normal_b_grad * normed_b, 0)
    mlp_shards = (
        lax.psum_scatter(
            up_grad.astype(jnp.bfloat16), ("dp", "fsdp"), scatter_dimension=0, tiled=True
        ).astype(jnp.float32),
        lax.psum_scatter(
            down_grad.astype(jnp.bfloat16), ("dp", "fsdp"), scatter_dimension=0, tiled=True
        ).astype(jnp.float32),
        lax.psum_scatter(
            ffn_gain_grad.astype(jnp.bfloat16), ("dp", "fsdp"), scatter_dimension=0, tiled=True
        ).astype(jnp.float32),
    )
    residual_grad = cotangent_rows.astype(jnp.float32) + norm_back(
        normal_b_grad, normed_b, inverse_b, ffn_gain
    )
    residual_low = residual_grad.astype(jnp.bfloat16)
    out_grad = outer_sum(attended_flat, residual_low)
    upstream_heads = (
        jnp.dot(residual_low, out_whole.T, preferred_element_type=jnp.float32)
        .astype(jnp.bfloat16)
        .reshape(head_shape)
    )
    delta_sum = jnp.transpose(
        jnp.sum(upstream_heads.astype(jnp.float32) * attended.astype(jnp.float32), -1), (0, 2, 1)
    )
    context_step = partial(
        gradient_step,
        query_heads=query_heads,
        upstream_heads=upstream_heads,
        log_total=log_total,
        delta_sum=delta_sum,
        score_scale=score_scale,
    )
    query_zero = jnp.zeros(head_shape, jnp.float32)
    whole_zero = jnp.zeros((2, seq_count, block_len * lax.axis_size("ctx"), D), jnp.float32)
    query_acc, key_whole = in_blocks(
        context_step,
        (query_zero, whole_zero),
        lax.all_gather(key_value, "ctx", axis=2, tiled=True),
        jnp.int32(0),
    )
    key_grads = lax.psum_scatter(
        key_whole.astype(jnp.bfloat16), "ctx", scatter_dimension=2, tiled=True
    ).astype(jnp.float32)
    query_grad = rotate_heads(query_acc, cosine_table, -sine_table)
    key_grad = rotate_heads(key_grads[0].reshape(head_shape), cosine_table, -sine_table)
    projected_grad = jnp.concatenate(
        [
            query_grad.reshape(row_count, D),
            key_grad.reshape(row_count, D),
            key_grads[1].reshape(row_count, D),
        ],
        -1,
    ).astype(jnp.bfloat16)
    qkv_grad = outer_sum(normal_a, projected_grad)
    normal_a_grad = jnp.dot(projected_grad, qkv_whole.T, preferred_element_type=jnp.float32)
    attn_gain_grad = jnp.sum(normal_a_grad * normed_a, 0)
    token_grad = residual_grad + norm_back(normal_a_grad, normed_a, inverse_a, attn_gain)
    attn_shards = (
        lax.psum_scatter(
            qkv_grad.astype(jnp.bfloat16), ("dp", "fsdp"), scatter_dimension=0, tiled=True
        ).astype(jnp.float32),
        lax.psum_scatter(
            out_grad.astype(jnp.bfloat16), ("dp", "fsdp"), scatter_dimension=0, tiled=True
        ).astype(jnp.float32),
        lax.psum_scatter(
            attn_gain_grad.astype(jnp.bfloat16), ("dp", "fsdp"), scatter_dimension=0, tiled=True
        ).astype(jnp.float32),
    )
    summed = (
        lax.psum(attn_shards[0].astype(jnp.bfloat16), "ctx").astype(jnp.float32),
        lax.psum(attn_shards[1].astype(jnp.bfloat16), "ctx").astype(jnp.float32),
        lax.psum(mlp_shards[0].astype(jnp.bfloat16), "ctx").astype(jnp.float32),
        lax.psum(mlp_shards[1].astype(jnp.bfloat16), "ctx").astype(jnp.float32),
        lax.psum(attn_shards[2].astype(jnp.bfloat16), "ctx").astype(jnp.float32),
        lax.psum(mlp_shards[2].astype(jnp.bfloat16), "ctx").astype(jnp.float32),
    )
    return (
        output.reshape(seq_count, block_len, D),
        token_grad.reshape(seq_count, block_len, D),
        summed[0],
        summed[1],
        summed[2],
        summed[3],
        summed[4],
        summed[5],
    )


def solution(mesh):
    placed = (
        P(("dp", "fsdp"), "ctx", None),
        P(("dp", "fsdp"), "ctx", None),
        P(("dp", "fsdp"), None),
        P(("dp", "fsdp"), None),
        P(("dp", "fsdp"), None),
        P(("dp", "fsdp"), None),
        P(("dp", "fsdp")),
        P(("dp", "fsdp")),
    )
    return jax.shard_map(
        body,
        mesh=mesh,
        in_specs=placed,
        out_specs=(
            P(("dp", "fsdp"), "ctx", None),
            P(("dp", "fsdp"), "ctx", None),
            P(("dp", "fsdp"), None),
            P(("dp", "fsdp"), None),
            P(("dp", "fsdp"), None),
            P(("dp", "fsdp"), None),
            P(("dp", "fsdp")),
            P(("dp", "fsdp")),
        ),
        check_vma=False,
    )
```

profile of v0, /device:TPU:0, one launch (start us, length us, event | category | flops | bytes accessed | tf_op | source)
XLA Modules:
  0.0 1381.8 jit_solution(6020721192050137913)
XLA Ops:
  11.6 15.7 %all-reduce.5 = (bf16[768]{0:T(1024)(128)(2,1)S(1)}, bf16[768]{0:T(1024)(128)(2,1)S(1)}) all-reduce(bf16[768]{0:T(1024)(128)(2,1)S(1)} %dynamic-update-slice, bf16[768]{0:T(1024)(128)(2,1)S(1)} %dynamic-update-slice.1), channel_id=1, replica_groups=mesh['dp'=4,'ctx'=4,'fsdp'=2] {'dp','fsdp'}, use_global_device_ids=true, to_apply=%add | all-reduce | flops 1536 | bytes 6144
  31.3 15.4 %all-gather.6.cloned.1.call-done = bf16[768,2304]{1,0:T(8,128)(2,1)} async-done(((bf16[96,2304]{1,0:T(8,128)(2,1)}), bf16[768,2304]{1,0:T(8,128)(2,1)}) %all-gather.6.cloned.1.call-update) | async-done | bytes 3538960 | tf_op jit(solution)/shard_map/all_gather | solution.py:145
  89.3 205.2 %all-gather.8.cloned.1.call-done = bf16[2,2,2048,768]{2,3,1,0:T(8,128)(2,1)} async-done(((bf16[2,2,512,768]{2,3,1,0:T(8,128)(2,1)}), bf16[2,2,2048,768]{2,3,1,0:T(8,128)(2,1)}) %all-gather.8.cloned.1.call-update) | async-done | bytes 12582928 | tf_op jit(solution)/shard_map/all_gather | solution.py:184
  294.6 143.1 %while.34 = (s32[]{:T(128)}, f32[2,12,512]{2,1,0:T(8,128)S(1)}, f32[2,12,512]{2,1,0:T(8,128)S(1)}, f32[2,12,512,64]{2,3,1,0:T(8,128)}, bf16[2,2,2048,768]{2,3,1,...) while((s32[]{:T(128)}, f32[2,12,512]{2,1,0:T(8,128)S(1)}, ...), condition=%wide.region_5.0_spmd.clone, body=%wide.region_2.0_spmd.clone.sunk | while | flops 1663365120 | bytes 118751480 | solution.py:69
  459.5 15.4 %add_convert_fusion = (bf16[1024,1152]{1,0:T(8,128)(2,1)S(1)}, f32[1024,1152]{1,0:T(8,128)S(1)}, f32[1024,1152]{1,0:T(8,128)S(1)}) fusion(f32[1024,2304]{1,0:T(8,128)} %fusion.55, bf16[1024,768]{1,0:T(8,128)(2,1)S(1)} %bitcast.199, bf16[1152,768]{1,0:T(8,128)(2,1)} %all-gather.14.cloned.1.call-done), kind=kOutput, calls=%fused_computation.38 | convolution fusion | flops 1898053632 | bytes 24576000 | tf_op jit(solution)/shard_map/dot_general | solution.py:200
  510.8 384.6 %while.35 = (s32[]{:T(128)}, f32[2,512,12,64]{1,3,2,0:T(8,128)}, f32[2,2,2048,768]{3,2,1,0:T(8,128)}, bf16[2,2,2048,768]{2,3,1,0:T(8,128)(2,1)}, bf16[2,512,12,6...) while((s32[]{:T(128)}, f32[2,512,12,64]{1,3,2,0:T(8,128)}, ...), condition=%wide.region_12.0_spmd.clone, body=%wide.region_11.0_spmd.clone.sunk | while | flops 4083154944 | bytes 250233200 | solution.py:69
  528.4 11.5 fusion.126
  539.9 12.2 fusion.127
  552.1 14.5 %multiply_convert_fusion.7 = bf16[2,12,512,512]{3,2,1,0:T(8,128)(2,1)} fusion(f32[2,12,512,512]{3,2,1,0:T(8,128)} %fusion.126, f32[2,12,512]{2,1,0:T(8,128)S(1)} %get-tuple-element.614, f32[2,12,512]{2,1,0:T(8,128)S(1)} %get-tuple-element.612, bf16[2,512,12,64]{1,3,2,0:T(8,128)(2,1)} %bitcast.179, bf16[2,512,12,64]{1,3,2,0:T(8,128)(2,1)S(1)} %get-tuple-element.613), kind=kOutput, calls=%fused_computation.17.clone.1 | convolution fusion | flops 836763648 | bytes 40992768 | tf_op jit(solution)/shard_map/while/body/eval_jaxpr/sbhd,srhd->shbr/dot_general | solution.py:107
  623.7 11.5 fusion.126
  635.2 12.2 fusion.127
  647.4 14.5 %multiply_convert_fusion.7 = bf16[2,12,512,512]{3,2,1,0:T(8,128)(2,1)} fusion(f32[2,12,512,512]{3,2,1,0:T(8,128)} %fusion.126, f32[2,12,512]{2,1,0:T(8,128)S(1)} %get-tuple-element.614, f32[2,12,512]{2,1,0:T(8,128)S(1)} %get-tuple-element.612, bf16[2,512,12,64]{1,3,2,0:T(8,128)(2,1)} %bitcast.179, bf16[2,512,12,64]{1,3,2,0:T(8,128)(2,1)S(1)} %get-tuple-element.613), kind=kOutput, calls=%fused_computation.17.clone.1 | convolution fusion | flops 836763648 | bytes 40992768 | tf_op jit(solution)/shard_map/while/body/eval_jaxpr/sbhd,srhd->shbr/dot_general | solution.py:107
  731.5 12.2 fusion.127
  743.7 14.5 %multiply_convert_fusion.7 = bf16[2,12,512,512]{3,2,1,0:T(8,128)(2,1)} fusion(f32[2,12,512,512]{3,2,1,0:T(8,128)} %fusion.126, f32[2,12,512]{2,1,0:T(8,128)S(1)} %get-tuple-element.614, f32[2,12,512]{2,1,0:T(8,128)S(1)} %get-tuple-element.612, bf16[2,512,12,64]{1,3,2,0:T(8,128)(2,1)} %bitcast.179, bf16[2,512,12,64]{1,3,2,0:T(8,128)(2,1)S(1)} %get-tuple-element.613), kind=kOutput, calls=%fused_computation.17.clone.1 | convolution fusion | flops 836763648 | bytes 40992768 | tf_op jit(solution)/shard_map/while/body/eval_jaxpr/sbhd,srhd->shbr/dot_general | solution.py:107
  827.7 12.2 fusion.127
  839.9 14.5 %multiply_convert_fusion.7 = bf16[2,12,512,512]{3,2,1,0:T(8,128)(2,1)} fusion(f32[2,12,512,512]{3,2,1,0:T(8,128)} %fusion.126, f32[2,12,512]{2,1,0:T(8,128)S(1)} %get-tuple-element.614, f32[2,12,512]{2,1,0:T(8,128)S(1)} %get-tuple-element.612, bf16[2,512,12,64]{1,3,2,0:T(8,128)(2,1)} %bitcast.179, bf16[2,512,12,64]{1,3,2,0:T(8,128)(2,1)S(1)} %get-tuple-element.613), kind=kOutput, calls=%fused_computation.17.clone.1 | convolution fusion | flops 836763648 | bytes 40992768 | tf_op jit(solution)/shard_map/while/body/eval_jaxpr/sbhd,srhd->shbr/dot_general | solution.py:107
  895.4 13.2 convert_element_type.163
  938.1 181.0 %reduce-scatter.6.cloned.1.call-done = bf16[2,2,512,768]{3,2,1,0:T(8,128)(2,1)} async-done(((bf16[2,2,2048,768]{3,2,1,0:T(8,128)(2,1)}), bf16[2,2,512,768]{3,2,1,0:T(8,128)(2,1)}) %reduce-scatter.6.cloned.1.call-update) | async-done | bytes 3145744 | tf_op jit(solution)/shard_map/reduce_scatter | solution.py:246
  1166.7 36.0 %reduce-scatter.14.cloned.1.call-done = bf16[144,768]{1,0:T(8,128)(2,1)} async-done(((bf16[1152,768]{1,0:T(8,128)(2,1)}), bf16[144,768]{1,0:T(8,128)(2,1)}) %reduce-scatter.14.cloned.1.call-update) | async-done | bytes 221200 | tf_op jit(solution)/shard_map/reduce_scatter | solution.py:210
  1202.7 51.5 %reduce-scatter.12.cloned.1.call-done = bf16[96,2304]{1,0:T(8,128)(2,1)} async-done(((bf16[768,2304]{1,0:T(8,128)(2,1)}), bf16[96,2304]{1,0:T(8,128)(2,1)}) %reduce-scatter.12.cloned.1.call-update) | async-done | bytes 442384 | tf_op jit(solution)/shard_map/reduce_scatter | solution.py:207
  1254.2 51.3 %reduce-scatter.8.cloned.1.call-done = bf16[96,2304]{1,0:T(8,128)(2,1)} async-done(((bf16[768,2304]{1,0:T(8,128)(2,1)}), bf16[96,2304]{1,0:T(8,128)(2,1)}) %reduce-scatter.8.cloned.1.call-update) | async-done | bytes 442384 | tf_op jit(solution)/shard_map/reduce_scatter | solution.py:264
  1314.6 14.1 %all-reduce.4 = (bf16[768]{0:T(1024)(128)(2,1)S(1)}, bf16[768]{0:T(1024)(128)(2,1)S(1)}) all-reduce(bf16[768]{0:T(1024)(128)(2,1)S(1)} %get-tuple-element.364, bf16[768]{0:T(1024)(128)(2,1)S(1)} %copy-done.48), channel_id=7, replica_groups=mesh['dp'=4,'ctx'=4,'fsdp'=2] {'dp','fsdp'}, use_global_device_ids=true, to_apply=%region_25.0.clone | all-reduce | flops 1536 | bytes 6144
  1328.8 11.6 all-reduce.6
  1346.0 21.5 %all-reduce.10.cloned.1.call-done = (bf16[96,2304]{1,0:T(8,128)(2,1)}, bf16[96,768]{1,0:T(8,128)(2,1)}, bf16[96,2304]{1,0:T(8,128)(2,1)}, bf16[144,768]{1,0:T(8,128)(2,1)}) async-done(((bf16[96,2304]{1,0:T(8,128)(2,1)}, bf16[96,768]{1,0:T(8,128)(2,1)}, bf16[96,2304]{1,0:T(8,128)(2,1)}, bf16[144,768]{1,0:T(8,128)(2,1)}), (bf16[96,2304]{1,0:T(8,128)(2,1)}, bf16[96,768]{1,0:T(8,128)(2,1)}, ...) | async-done | bytes 1253392 | tf_op jit(solution)/shard_map/psum | solution.py:275
  (331 shorter events, 602.3 us)
Async XLA Ops:
  7.2 39.5 %all-gather.6.cloned.1.call-start = ((), (), s32[]{:S(2)}) async-start(), calls=%async_computation.5 | async-start | bytes 3981312 | tf_op jit(solution)/shard_map/all_gather | solution.py:145
  7.9 286.7 %all-gather.8.cloned.1.call-start = ((), (), s32[]{:S(2)}) async-start(), calls=%async_computation.6 | async-start | bytes 15728640 | tf_op jit(solution)/shard_map/all_gather | solution.py:184
  30.7 40.3 %copy-start.33 = (f32[512,64]{0,1:T(8,128)}, f32[512,64]{0,1:T(8,128)S(1)}, u32[]{:S(2)}) copy-start(f32[512,64]{0,1:T(8,128)S(1)} %get-tuple-element.433) | copy-start | bytes 393220
  30.7 55.9 %copy-start.24 = (f32[512,64]{0,1:T(8,128)}, f32[512,64]{0,1:T(8,128)S(1)}, u32[]{:S(2)}) copy-start(f32[512,64]{0,1:T(8,128)S(1)} %get-tuple-element.445) | copy-start | bytes 393220
  76.2 367.0 %all-gather.10.cloned.1.call-start = ((), (), s32[]{:S(2)}) async-start(), calls=%async_computation.7 | async-start | bytes 1327104 | tf_op jit(solution)/shard_map/all_gather | solution.py:146
  77.0 371.8 %all-gather.12.cloned.1.call-start = ((), (), s32[]{:S(2)}) async-start(), calls=%async_computation.8 | async-start | bytes 3981312 | tf_op jit(solution)/shard_map/all_gather | solution.py:147
  77.5 382.0 %all-gather.14.cloned.1.call-start = ((), (), s32[]{:S(2)}) async-start(), calls=%async_computation.9 | async-start | bytes 1990656 | tf_op jit(solution)/shard_map/all_gather | solution.py:148
  78.1 1040.9 %reduce-scatter.6.cloned.1.call-start = ((), (), s32[]{:S(2)}) async-start(), calls=%async_computation.10 | async-start | bytes 15728640 | tf_op jit(solution)/shard_map/reduce_scatter | solution.py:246
  78.2 407.4 %copy-start.44 = (f32[768]{0:T(1024)}, f32[768]{0:T(1024)S(1)}, u32[]{:S(2)}) copy-start(f32[768]{0:T(1024)S(1)} %convert_element_type.154) | copy-start | bytes 9220
  446.6 39.1 %copy-start.42 = (f32[1024]{0:T(1024)}, f32[1024]{0:T(1024)S(1)}, u32[]{:S(2)}) copy-start(f32[1024]{0:T(1024)S(1)} %broadcast_multiply_fusion.4) | copy-start | bytes 12292
  448.7 36.9 %copy-start.46 = (f32[1024]{0:T(1024)}, f32[1024]{0:T(1024)S(1)}, u32[]{:S(2)}) copy-start(f32[1024]{0:T(1024)S(1)} %add_rsqrt_fusion) | copy-start | bytes 12292
  511.2 40.9 %copy-start.4 = (bf16[2,512,12,64]{1,3,2,0:T(8,128)(2,1)}, bf16[2,512,12,64]{1,3,2,0:T(8,128)(2,1)S(1)}, u32[]{:S(2)}) copy-start(bf16[2,512,12,64]{1,3,2,0:T(8,128)(2,1)S(1)} %get-tuple-element.613) | copy-start | bytes 4718596 | tf_op jit(solution)/shard_map/while
  606.4 41.0 %copy-start.4 = (bf16[2,512,12,64]{1,3,2,0:T(8,128)(2,1)}, bf16[2,512,12,64]{1,3,2,0:T(8,128)(2,1)S(1)}, u32[]{:S(2)}) copy-start(bf16[2,512,12,64]{1,3,2,0:T(8,128)(2,1)S(1)} %get-tuple-element.613) | copy-start | bytes 4718596 | tf_op jit(solution)/shard_map/while
  702.8 40.9 %copy-start.4 = (bf16[2,512,12,64]{1,3,2,0:T(8,128)(2,1)}, bf16[2,512,12,64]{1,3,2,0:T(8,128)(2,1)S(1)}, u32[]{:S(2)}) copy-start(bf16[2,512,12,64]{1,3,2,0:T(8,128)(2,1)S(1)} %get-tuple-element.613) | copy-start | bytes 4718596 | tf_op jit(solution)/shard_map/while
  799.1 40.9 %copy-start.4 = (bf16[2,512,12,64]{1,3,2,0:T(8,128)(2,1)}, bf16[2,512,12,64]{1,3,2,0:T(8,128)(2,1)S(1)}, u32[]{:S(2)}) copy-start(bf16[2,512,12,64]{1,3,2,0:T(8,128)(2,1)S(1)} %get-tuple-element.613) | copy-start | bytes 4718596 | tf_op jit(solution)/shard_map/while
  908.6 258.1 %reduce-scatter.10.cloned.1.call-start = ((), (), s32[]{:S(2)}) async-start(), calls=%async_computation.12 | async-start | bytes 1327104 | tf_op jit(solution)/shard_map/reduce_scatter | solution.py:267
  914.3 288.4 %reduce-scatter.14.cloned.1.call-start = ((), (), s32[]{:S(2)}) async-start(), calls=%async_computation.14 | async-start | bytes 1990656 | tf_op jit(solution)/shard_map/reduce_scatter | solution.py:210
  920.0 334.2 %reduce-scatter.12.cloned.1.call-start = ((), (), s32[]{:S(2)}) async-start(), calls=%async_computation.13 | async-start | bytes 3981312 | tf_op jit(solution)/shard_map/reduce_scatter | solution.py:207
  928.3 377.1 %reduce-scatter.8.cloned.1.call-start = ((), (), s32[]{:S(2)}) async-start(), calls=%async_computation.11 | async-start | bytes 3981312 | tf_op jit(solution)/shard_map/reduce_scatter | solution.py:264
  1159.4 208.1 %all-reduce.10.cloned.1.call-start = ((), (), s32[]{:S(2)}) async-start(), calls=%async_computation.15 | async-start | bytes 2506752 | tf_op jit(solution)/shard_map/psum | solution.py:275
  1160.1 145.4 %copy-start.10 = (bf16[2,512,768]{2,1,0:T(8,128)(2,1)S(1)}, bf16[2,512,768]{2,1,0:T(8,128)(2,1)}, u32[]{:S(2)}) copy-start(bf16[2,512,768]{2,1,0:T(8,128)(2,1)} %param.12) | copy-start | bytes 4718596
  1160.1 145.4 %copy-start.37 = (f32[768]{0:T(1024)S(1)}, f32[768]{0:T(1024)}, u32[]{:S(2)}) copy-start(f32[768]{0:T(1024)} %copy-done.36) | copy-start | bytes 9220
  1160.1 145.4 %copy-start.39 = (f32[1,4,2,128]{3,1,2,0:T(4,128)S(1)}, f32[1,4,2,128]{3,1,2,0:T(4,128)}, u32[]{:S(2)}) copy-start(f32[1,4,2,128]{3,1,2,0:T(4,128)} %copy-done.38) | copy-start | bytes 12292
  1160.1 145.4 %copy-start.41 = (f32[1,4,2,128]{3,1,2,0:T(4,128)S(1)}, f32[1,4,2,128]{3,1,2,0:T(4,128)}, u32[]{:S(2)}) copy-start(f32[1,4,2,128]{3,1,2,0:T(4,128)} %copy-done.40) | copy-start | bytes 12292
  (62 other events, 396.1 us)
Sparse Core Ops, SparseCore 0:
  9.9 36.7 all-gather.5
  76.4 218.1 all-gather.7
  296.5 22.0 all-gather.9
  320.3 33.8 all-gather.11
  355.9 26.3 all-gather.13
  908.7 210.3 reduce-scatter.5
  1122.3 37.7 reduce-scatter.9
  1163.4 39.2 reduce-scatter.13
  1206.2 47.9 reduce-scatter.11
  1257.5 47.9 reduce-scatter.7
  1308.2 59.3 all-reduce.9
where the time goes:
time: 1390 us; the launch traced here: 1380 us
  waiting for transfers between devices  564 us (41%)
  matrix products  401 us (29%)
  local copies, waits for them, and re-layouts  214 us (15%)
  other arithmetic  142 us (10%)
  blocking collectives  41.3 us (3%)
  between operations  16.5 us (1%)
    all_gather x1, waiting for transfers between devices, body(): lax.all_gather(key_value, 'ctx', axis=2, tiled=True)  205 us
    reduce_scatter x1, waiting for transfers between devices, body(): lax.psum_scatter(key_whole.astype(jnp.bfloat16), 'ctx', scatter_dimension...  181 us
    dot_general x4, matrix products, gradient_step(): jnp.einsum('sbhd,srhd->shbr', upstream_heads, value_heads, preferred_elem...  58.2 us
    reduce_scatter x1, waiting for transfers between devices, body(): lax.psum_scatter(up_grad.astype(jnp.bfloat16), ('dp', 'fsdp'), scatter_di...  51.5 us
    dynamic_update_slice x8, local copies, waits for them, and re-layouts, gradient_step(): lax.dynamic_update_slice_in_dim(key_acc, earlier + both_terms, first_row, 2)  51.4 us
    reduce_scatter x1, waiting for transfers between devices, body(): lax.psum_scatter(qkv_grad.astype(jnp.bfloat16), ('dp', 'fsdp'), scatter_d...  51.3 us
    dynamic_slice x8, local copies, waits for them, and re-layouts, gradient_step(): lax.dynamic_slice_in_dim(key_acc, first_row, key_block.shape[2], 2)  50.7 us
    dot_general x4, matrix products, gradient_step(): jnp.einsum('shbr,sbhd->srhd', weights.astype(jnp.bfloat16), upstream_head...  48.8 us
  transfers between devices with their start and end apart: 11, of which 7 were waited for; matrix products, arithmetic and copies ran while one was open for 19% of the time, Pallas kernels for 0%

commit v1 on v0

v1 whole, which is shorter than its diff:
```python
from functools import partial
import math

import jax
import jax.numpy as jnp
from jax import lax
from jax.experimental import pallas as pl
from jax.experimental.pallas import tpu as pltpu
from jax.sharding import PartitionSpec as P

D = 768
HEADS = 12
HEAD = 64
FF = 1152
HALF = HEAD // 2

norm_eps = 1e-05
rope_base = 160000.0
score_scale = HEAD ** (-0.5)
score_base2 = score_scale * math.log2(math.e)
WEIGHT_AXES = ("dp", "fsdp")
f32 = jnp.float32
bf16 = jnp.bfloat16


def dot(left, right, left_dim=1, right_dim=0):
    return lax.dot_general(
        left, right, (((left_dim,), (right_dim,)), ((), ())), preferred_element_type=f32
    )


def layer_norm(values, norm_gain):
    centre = jnp.mean(values, -1, keepdims=True)
    centred = values - centre
    inverse = lax.rsqrt(jnp.mean(centred * centred, -1, keepdims=True) + norm_eps)
    normed = centred * inverse
    return (normed, inverse, normed * norm_gain)


def norm_back(upstream, normed, inverse, norm_gain):
    scaled = upstream * norm_gain
    return (
        scaled
        - jnp.mean(scaled, -1, keepdims=True)
        - normed * jnp.mean(scaled * normed, -1, keepdims=True)
    ) * inverse


def gated_gelu(inputs, gating):
    return jax.nn.gelu(inputs, approximate=False) * gating


def rope_rows(length):
    frequency = rope_base ** (-2.0 * jnp.arange(HALF, dtype=f32) / HEAD)
    angles = frequency[:, None] * jnp.arange(length, dtype=jnp.int32).astype(f32)[None, :]
    return (jnp.cos(angles), jnp.sin(angles))


def chunk_of(length, most):
    return most if length % most == 0 else length


def forward_kernel(q_ref, k_ref, v_ref, o_ref, log_ref, k_rows, v_wide):
    length = k_ref.shape[-1]
    chunk = chunk_of(length, 512)

    @pl.when(pl.program_id(1) == 0)
    def _():
        k_rows[...] = k_ref[0, 0].T
        v_wide[:HEAD, :] = v_ref[0, 0]
        v_wide[HEAD:, :] = jnp.ones((v_wide.shape[0] - HEAD, length), bf16)

    query = q_ref[0, 0]
    highest = None
    total = None
    for start in range(0, length, chunk):
        scores = dot(k_rows[start : start + chunk, :], query) * score_base2
        top = jnp.max(scores, 0, keepdims=True)
        new_high = top if highest is None else jnp.maximum(highest, top)
        weights = jnp.exp2(scores - new_high).astype(bf16)
        term = dot(v_wide[:, start : start + chunk], weights)
        total = term if total is None else total * jnp.exp2(highest - new_high) + term
        highest = new_high
    denominator = total[HEAD : HEAD + 1, :]
    o_ref[0, 0] = (total[:HEAD, :] / denominator).astype(bf16)
    log_ref[0] = highest + jnp.log2(denominator)


def attend(heads_t, block_len):
    _, count, _, length = heads_t.shape
    blocks = length // block_len
    return pl.pallas_call(
        forward_kernel,
        grid=(count, blocks),
        in_specs=[
            pl.BlockSpec((1, 1, HEAD, block_len), lambda h, c: (0, h, 0, c)),
            pl.BlockSpec((1, 1, HEAD, length), lambda h, c: (1, h, 0, 0)),
            pl.BlockSpec((1, 1, HEAD, length), lambda h, c: (2, h, 0, 0)),
        ],
        out_specs=[
            pl.BlockSpec((1, 1, HEAD, block_len), lambda h, c: (c, h, 0, 0)),
            pl.BlockSpec((1, 1, block_len), lambda h, c: (h, 0, c)),
        ],
        out_shape=[
            jax.ShapeDtypeStruct((blocks, count, HEAD, block_len), bf16),
            jax.ShapeDtypeStruct((count, 1, length), f32),
        ],
        scratch_shapes=[
            pltpu.VMEM((length, HEAD), bf16),
            pltpu.VMEM((HEAD + 16, length), bf16),
        ],
        compiler_params=pltpu.CompilerParams(vmem_limit_bytes=40 << 20),
        cost_estimate=pl.CostEstimate(
            flops=16 * count * length * length * HEAD,
            bytes_accessed=10 * count * length * HEAD,
            transcendentals=count * length * length,
        ),
    )(heads_t, heads_t, heads_t)


def rope_back(grad_t, cosine, sine):
    first, second = grad_t[:HALF, :], grad_t[HALF:, :]
    return (first * cosine + second * sine, second * cosine - first * sine)


def backward_kernel(
    q_ref, k_ref, v_ref, o_ref, up_ref, log_ref, cos_all, sin_all, cos_ref, sin_ref,
    dq_ref, dk_ref, dv_ref, q_rows, up_rows, up_cols, delta, dq_sum,
):
    step = pl.program_id(1)
    blocks, block_len = up_ref.shape[0], up_ref.shape[-1]
    length = q_ref.shape[-1]
    chunk = chunk_of(length, 512)

    @pl.when(step == 0)
    def _():
        q_rows[...] = q_ref[0, 0].T
        for number in range(blocks):
            place = slice(number * block_len, (number + 1) * block_len)
            upstream = up_ref[number, 0]
            up_cols[:, place] = upstream
            up_rows[place, :] = upstream.T
            delta[:, place] = jnp.sum(
                upstream.astype(f32) * o_ref[number, 0].astype(f32), 0, keepdims=True
            )
        dq_sum[...] = jnp.zeros_like(dq_sum)

    key_t = k_ref[0, 0]
    key = key_t.T
    value = v_ref[0, 0].T
    dk = None
    dv = None
    for start in range(0, length, chunk):
        place = slice(start, start + chunk)
        scores = dot(key, q_ref[0, 0, :, place]) * score_base2
        weights = jnp.exp2(scores - log_ref[0, :, place])
        weight_grad = dot(value, up_cols[:, place])
        score_grad = (weights * (weight_grad - delta[:, place])).astype(bf16)
        dv_term = dot(weights.astype(bf16), up_rows[place, :])
        dk_term = dot(score_grad, q_rows[place, :])
        dv = dv_term if dv is None else dv + dv_term
        dk = dk_term if dk is None else dk + dk_term
        dq_sum[:, place] += dot(key_t, score_grad)
    upper, lower = rope_back((dk * score_scale).T, cos_ref[...], sin_ref[...])
    dk_ref[0, :HALF, :] = upper.astype(bf16)
    dk_ref[0, HALF:, :] = lower.astype(bf16)
    dv_ref[0] = dv.T.astype(bf16)

    @pl.when(step == pl.num_programs(1) - 1)
    def _():
        upper, lower = rope_back(dq_sum[...] * score_scale, cos_all[...], sin_all[...])
        dq_ref[0, :HALF, :] = upper.astype(bf16)
        dq_ref[0, HALF:, :] = lower.astype(bf16)


def attend_back(heads_t, attended, upstream, log_total, cosine, sine):
    _, count, _, length = heads_t.shape
    blocks, _, _, block_len = attended.shape
    rows = chunk_of(length, 256)
    split = pl.BlockSpec((blocks, 1, HEAD, block_len), lambda h, k: (0, h, 0, 0))
    shape = jax.ShapeDtypeStruct((count, HEAD, length), bf16)
    return pl.pallas_call(
        backward_kernel,
        grid=(count, length // rows),
        in_specs=[
            pl.BlockSpec((1, 1, HEAD, length), lambda h, k: (0, h, 0, 0)),
            pl.BlockSpec((1, 1, HEAD, rows), lambda h, k: (1, h, 0, k)),
            pl.BlockSpec((1, 1, HEAD, rows), lambda h, k: (2, h, 0, k)),
            split,
            split,
            pl.BlockSpec((1, 1, length), lambda h, k: (h, 0, 0)),
            pl.BlockSpec((HALF, length), lambda h, k: (0, 0)),
            pl.BlockSpec((HALF, length), lambda h, k: (0, 0)),
            pl.BlockSpec((HALF, rows), lambda h, k: (0, k)),
            pl.BlockSpec((HALF, rows), lambda h, k: (0, k)),
        ],
        out_specs=[
            pl.BlockSpec((1, HEAD, length), lambda h, k: (h, 0, 0)),
            pl.BlockSpec((1, HEAD, rows), lambda h, k: (h, 0, k)),
            pl.BlockSpec((1, HEAD, rows), lambda h, k: (h, 0, k)),
        ],
        out_shape=[shape, shape, shape],
        scratch_shapes=[
            pltpu.VMEM((length, HEAD), bf16),
            pltpu.VMEM((length, HEAD), bf16),
            pltpu.VMEM((HEAD, length), bf16),
            pltpu.VMEM((1, length), f32),
            pltpu.VMEM((HEAD, length), f32),
        ],
        compiler_params=pltpu.CompilerParams(vmem_limit_bytes=40 << 20),
        cost_estimate=pl.CostEstimate(
            flops=40 * count * length * length * HEAD,
            bytes_accessed=16 * count * length * HEAD,
            transcendentals=count * length * length,
        ),
    )(heads_t, heads_t, heads_t, attended, upstream, log_total, cosine, sine, cosine, sine)


def gather_rows(shard):
    return lax.all_gather(shard, WEIGHT_AXES, axis=0, tiled=True)


def exchange(blocks):
    return lax.all_to_all(blocks, "ctx", 0, 0, tiled=True)


def body(
    tokens,
    cotangent,
    qkv_weight,
    out_weight,
    up_weight,
    down_weight,
    attention_gain,
    feedforward_gain,
):
    ctx = lax.axis_size("ctx")
    groups = lax.axis_size("dp") * lax.axis_size("fsdp")
    seq_count, block_len = (tokens.shape[0], tokens.shape[1])
    length = block_len * ctx
    own = -(-HEADS // ctx)
    width = own * HEAD
    spare = ctx * own - HEADS
    shard_rows = qkv_weight.shape[0]
    by_head = qkv_weight.reshape(shard_rows, 3, D)
    if spare:
        by_head = jnp.pad(by_head, ((0, 0), (0, 0), (0, spare * HEAD)))
    own_columns = lax.dynamic_slice_in_dim(by_head, lax.axis_index("ctx") * width, width, 2)
    gains = gather_rows(jnp.stack([attention_gain, feedforward_gain], -1)).astype(f32)
    attn_gain, ffn_gain = (gains[:, 0], gains[:, 1])
    qkv_own = gather_rows(own_columns.reshape(shard_rows, 3 * width))
    gathered = [
        lax.all_gather(tokens[number], "ctx", axis=0, tiled=True) for number in range(seq_count)
    ]
    out_whole = gather_rows(out_weight)
    up_whole = gather_rows(up_weight)
    down_whole = gather_rows(down_weight)
    cosine, sine = rope_rows(length)

    saved = []
    for number in range(seq_count):
        normal = layer_norm(gathered[number].astype(f32), attn_gain)[2].astype(bf16)
        projected = dot(qkv_own, normal, 0, 1).reshape(3, own, 2, HALF, length)
        first, second = (projected[:2, :, 0], projected[:2, :, 1])
        turned = jnp.stack([first * cosine - second * sine, second * cosine + first * sine], 2)
        heads_t = (
            jnp.concatenate([turned, projected[2:]], 0).astype(bf16).reshape(3, own, HEAD, length)
        )
        attended, log_total = attend(heads_t, block_len)
        saved.append((normal, heads_t, attended, log_total, exchange(attended)))

    outputs = []
    middle = []
    up_grad = down_grad = out_grad = 0.0
    for number in range(seq_count):
        attended_t = saved[number][4].reshape(ctx * width, block_len)[:D]
        inputs = tokens[number].astype(f32)
        residual = inputs + dot(attended_t, out_whole, 0, 0)
        normed_b, inverse_b, scaled_b = layer_norm(residual, ffn_gain)
        normal_b = scaled_b.astype(bf16)
        widened = dot(normal_b, up_whole)
        hidden, hidden_back = jax.vjp(gated_gelu, widened[:, :FF], widened[:, FF:])
        hidden_low = hidden.astype(bf16)
        outputs.append((residual + dot(hidden_low, down_whole)).astype(bf16))
        upstream = cotangent[number]
        hidden_grad = dot(upstream, down_whole, 1, 1)
        input_grad, gating_grad = hidden_back(hidden_grad)
        widened_grad = jnp.concatenate([input_grad, gating_grad], -1).astype(bf16)
        normal_b_grad = dot(widened_grad, up_whole, 1, 1)
        residual_grad = upstream.astype(f32) + norm_back(
            normal_b_grad, normed_b, inverse_b, ffn_gain
        )
        residual_low = residual_grad.astype(bf16)
        attended_grad = dot(out_whole, residual_low, 1, 1).astype(bf16)
        if spare:
            attended_grad = jnp.pad(attended_grad, ((0, spare * HEAD), (0, 0)))
        middle.append(
            (residual_grad, exchange(attended_grad.reshape(ctx, own, HEAD, block_len)))
        )
        down_grad = down_grad + dot(hidden_low, upstream, 0, 0)
        up_grad = up_grad + dot(normal_b, widened_grad, 0, 0)
        out_grad = out_grad + dot(attended_t, residual_low)

    parts = [up_grad[:, start : start + D] for start in range(0, up_grad.shape[1], D)]
    parts += [down_grad, out_grad]
    packed = jnp.concatenate([part.astype(bf16).reshape(groups, -1, D) for part in parts], 1)
    shard = lax.psum_scatter(packed, WEIGHT_AXES, scatter_dimension=0, tiled=True)[0]
    shard = lax.psum(shard, "ctx").astype(f32)
    cuts = []
    offset = 0
    for part in parts:
        rows = part.shape[0] // groups
        cuts.append(shard[offset : offset + rows])
        offset += rows
    up_shard = jnp.concatenate(cuts[:-2], -1)
    down_shard, out_shard = cuts[-2:]

    token_grads = []
    qkv_grad = 0.0
    for number in range(seq_count):
        normal, heads_t, attended, log_total, _ = saved[number]
        residual_grad, upstream_t = middle[number]
        pieces = attend_back(heads_t, attended, upstream_t, log_total, cosine, sine)
        projected_grad = jnp.concatenate(pieces, 0).reshape(3 * width, length)
        partial_grad = dot(projected_grad, qkv_own, 0, 1).astype(bf16)
        normal_a_grad = lax.psum_scatter(
            partial_grad, "ctx", scatter_dimension=0, tiled=True
        ).astype(f32)
        qkv_grad = qkv_grad + dot(normal, projected_grad, 0, 1)
        normed_a, inverse_a, _ = layer_norm(tokens[number].astype(f32), attn_gain)
        token_grads.append(
            residual_grad + norm_back(normal_a_grad, normed_a, inverse_a, attn_gain)
        )
    qkv_cut = lax.psum_scatter(
        qkv_grad.astype(bf16), WEIGHT_AXES, scatter_dimension=0, tiled=True
    )
    qkv_all = lax.all_gather(qkv_cut, "ctx", axis=0).astype(f32)
    qkv_shard = jnp.transpose(qkv_all.reshape(ctx, shard_rows, 3, width), (1, 2, 0, 3)).reshape(
        shard_rows, 3, ctx * width
    )[:, :, :D].reshape(shard_rows, 3 * D)
    attn_gain_grad = jnp.sum(qkv_weight.astype(f32) * qkv_shard, -1) / attention_gain.astype(f32)
    ffn_gain_grad = jnp.sum(up_weight.astype(f32) * up_shard, -1) / feedforward_gain.astype(f32)
    return (
        jnp.stack(outputs),
        jnp.stack(token_grads),
        qkv_shard,
        out_shard,
        up_shard,
        down_shard,
        attn_gain_grad,
        ffn_gain_grad,
    )


def solution(mesh):
    rows = P(("dp", "fsdp"), "ctx", None)
    weight = P(("dp", "fsdp"), None)
    gain = P(("dp", "fsdp"))
    return jax.shard_map(
        body,
        mesh=mesh,
        in_specs=(rows, rows, weight, weight, weight, weight, gain, gain),
        out_specs=(rows, rows, weight, weight, weight, weight, gain, gain),
        check_vma=False,
    )
```

time: 1390 us -> 715 us (0.51)
  matrix products: 401 us -> 88 us
  waiting for transfers between devices: 564 us -> 319 us
  local copies, waits for them, and re-layouts: 214 us -> 48.5 us
  Pallas kernels: 0 us -> 132 us
  other arithmetic: 142 us -> 33.4 us
  starting transfers between devices: 0.44 us -> 18.2 us
  blocking collectives: 41.3 us -> 56.1 us
    dot_general x40 -> x24, matrix products: 401 us -> 88 us  [dot(): lax.dot_general(left, right, (((left_dim,), (right_dim,)), ((), ())), pre...]
    reduce_scatter x5 -> x4, waiting for transfers between devices: 320 us -> 163 us  [the longest x2 99 us: body(): lax.psum_scatter(partial_grad, 'ctx', scatter_dimension=0, tiled=True)]
    all_gather x5, waiting for transfers between devices: 221 us -> 81.7 us  [the longest x2 81.7 us: body(): lax.all_gather(tokens[number], 'ctx', axis=0, tiled=True)]
    pallas_call x0 -> x4, Pallas kernels: none -> 132 us  [the longest x2 82.7 us: attend_back(): pl.pallas_call(backward_kernel, grid=(count, length // rows), in_specs=[p...]
    all_gather x0 -> x3, blocking collectives: none -> 56.1 us  [the longest x2 34.4 us: gather_rows(): return lax.all_gather(shard, WEIGHT_AXES, axis=0, tiled=True)]
    dynamic_update_slice x8 -> x0, local copies, waits for them, and re-layouts: 51.4 us -> none  [gradient_step(): lax.dynamic_update_slice_in_dim(key_acc, earlier + both_terms, first_row, 2)]
    dynamic_slice x8 -> x2, local copies, waits for them, and re-layouts: 50.7 us -> 0.38 us  [body(): lax.dynamic_slice_in_dim(by_head, lax.axis_index('ctx') * width, width, 2)]
    reduce_sum x5 -> x3, other arithmetic: 45.4 us -> 5.18 us  [the longest x1 2.5 us: norm_back(): jnp.mean(scaled * normed, -1, keepdims=True)]
  transfers between devices with their start and end apart: 11 -> 14, of which waited for: 7 -> 8; matrix products, arithmetic and copies ran while one was open for 19% -> 13% of each run, Pallas kernels for 0% -> 13%
where the time goes in v1:
time: 715 us; the launch traced here: 710 us
  waiting for transfers between devices  319 us (45%)
  Pallas kernels  132 us (18%)
  matrix products  88 us (12%)
  blocking collectives  56.1 us (8%)
  local copies, waits for them, and re-layouts  48.5 us (7%)
  other arithmetic  33.4 us (5%)
  starting transfers between devices  18.2 us (3%)
  between operations  15.3 us (2%)
    reduce_scatter x2, waiting for transfers between devices, body(): lax.psum_scatter(partial_grad, 'ctx', scatter_dimension=0, tiled=True)  99 us
    dot_general x24, matrix products, dot(): lax.dot_general(left, right, (((left_dim,), (right_dim,)), ((), ())), pre...  88 us
    pallas_call x2, Pallas kernels, attend_back(): pl.pallas_call(backward_kernel, grid=(count, length // rows), in_specs=[p...  82.7 us
    all_gather x2, waiting for transfers between devices, body(): lax.all_gather(tokens[number], 'ctx', axis=0, tiled=True)  81.7 us
    reduce_scatter x1, waiting for transfers between devices, body(): lax.psum_scatter(packed, WEIGHT_AXES, scatter_dimension=0, tiled=True)[0]  63.6 us
    pallas_call x2, Pallas kernels, attend(): pl.pallas_call(forward_kernel, grid=(count, blocks), in_specs=[pl.BlockSp...  48.9 us
    psum x1, waiting for transfers between devices, body(): shard = lax.psum(shard, 'ctx').astype(f32)  42.3 us
    all_gather x2, blocking collectives, gather_rows(): return lax.all_gather(shard, WEIGHT_AXES, axis=0, tiled=True)  34.4 us
  transfers between devices with their start and end apart: 14, of which 8 were waited for; matrix products, arithmetic and copies ran while one was open for 13% of the time, Pallas kernels for 13%

profile of v1, /device:TPU:0, one launch (start us, length us, event | category | flops | bytes accessed | tf_op | source)
XLA Modules:
  0.0 709.9 jit_solution(3921878602464638867)
XLA Ops:
  13.3 21.0 %all_gather.27 = bf16[768,576]{1,0:T(8,128)(2,1)S(1)} all-gather(bf16[96,576]{1,0:T(8,128)(2,1)S(1)} %copy.46), channel_id=1, replica_groups=mesh['dp'=4,'ctx'=4,'fsdp'=2] {'dp','fsdp'}, dimensions={0}, use_global_device_ids=true | all-gather | bytes 995328 | tf_op jit(solution)/shard_map/all_gather | solution.py:220
  34.4 13.4 %all-gather.3 = bf16[8,96,2]{1,2,0:T(2,128)(2,1)S(1)} all-gather(bf16[1,96,2]{1,2,0:T(2,128)(2,1)S(1)} %maximum_bitcast_fusion), channel_id=1, replica_groups=mesh['dp'=4,'ctx'=4,'fsdp'=2] {'dp','fsdp'}, dimensions={0}, use_global_device_ids=true | all-gather | bytes 3456 | tf_op jit(solution)/shard_map/all_gather | solution.py:220
  48.9 27.4 %all-gather.18.cloned.1.call-done = bf16[1,2048,768]{2,1,0:T(8,128)(2,1)} async-done(((bf16[1,512,768]{2,1,0:T(8,128)(2,1)}), bf16[1,2048,768]{2,1,0:T(8,128)(2,1)}) %all-gather.18.cloned.1.call-update) | async-done | bytes 3145744 | tf_op jit(solution)/shard_map/all_gather | solution.py:253
  86.3 54.3 %all-gather.16.cloned.1.call-done = bf16[1,2048,768]{2,1,0:T(8,128)(2,1)} async-done(((bf16[1,512,768]{2,1,0:T(8,128)(2,1)}), bf16[1,2048,768]{2,1,0:T(8,128)(2,1)}) %all-gather.16.cloned.1.call-update) | async-done | bytes 3145744 | tf_op jit(solution)/shard_map/all_gather | solution.py:253
  151.2 24.6 %shard_map.144 = (bf16[4,3,64,512]{3,2,1,0:T(8,128)(2,1)S(1)}, f32[3,1,2048]{2,1,0:T(1,128)S(1)}) custom-call(bf16[3,3,64,2048]{3,2,1,0:T(8,128)(2,1)S(1)} %pad_maximum_fusion.2.q_ref.k_ref.v_ref, bf16[3,3,64,2048]{3,2,1,0:T(8,128)(2,1)S(1)} %pad_maximum_fusion.2.q_ref.k_ref.v_ref, bf16[3,3,64,2048]{3,2,1,0:T(8,128)(2,1)S(1)} %pad_maximum_fusion.2.q_ref.k_ref.v_ref), custom_call_target="tpu_custom_call" | custom-call | flops 12884901888 | bytes 3932160 | tf_op jit(solution)/shard_map/pallas_call | solution.py:92
  176.6 4.2 all-to-all-start.1
  182.7 24.3 %shard_map.143 = (bf16[4,3,64,512]{3,2,1,0:T(8,128)(2,1)S(1)}, f32[3,1,2048]{2,1,0:T(1,128)S(1)}) custom-call(bf16[3,3,64,2048]{3,2,1,0:T(8,128)(2,1)S(1)} %pad_maximum_fusion.1.q_ref.k_ref.v_ref, bf16[3,3,64,2048]{3,2,1,0:T(8,128)(2,1)S(1)} %pad_maximum_fusion.1.q_ref.k_ref.v_ref, bf16[3,3,64,2048]{3,2,1,0:T(8,128)(2,1)S(1)} %pad_maximum_fusion.1.q_ref.k_ref.v_ref), custom_call_target="tpu_custom_call" | custom-call | flops 12884901888 | bytes 3932160 | tf_op jit(solution)/shard_map/pallas_call | solution.py:92
  209.3 5.0 all-to-all-start
  218.4 15.7 %all-to-all-done = bf16[4,3,64,512]{3,2,1,0:T(8,128)(2,1)} async-done(((bf16[4,3,64,512]{3,2,1,0:T(8,128)(2,1)}), bf16[4,3,64,512]{3,2,1,0:T(8,128)(2,1)}, u32[]{:S(2)}, u32[]{:S(2)}) %all-to-all-start) | async-done | bytes 786464 | tf_op jit(solution)/shard_map/all_to_all | solution.py:224
  238.3 6.7 fusion.82
  245.0 19.3 %add_convert_fusion.3 = (bf16[512,1152]{1,0:T(8,128)(2,1)S(1)}, f32[512,1152]{1,0:T(8,128)S(1)}, f32[512,1152]{1,0:T(8,128)S(1)}) fusion(f32[512,2304]{1,0:T(8,128)} %fusion.82, bf16[1152,768]{1,0:T(8,128)(2,1)} %all-gather.14.cloned.1.call-done, bf16[2,512,768]{2,1,0:T(8,128)(2,1)} %param.9), kind=kOutput, calls=%fused_computation.36 | convolution fusion | flops 949026816 | bytes 13172736 | tf_op jit(solution)/shard_map/dot_general | solution.py:27
  272.5 6.1 add_convert_fusion.2
  289.8 4.2 all-to-all-start.2
  299.8 13.9 %all-to-all-done.2.up_ref = bf16[4,3,64,512]{3,2,1,0:T(8,128)(2,1)} async-done(((bf16[4,3,64,512]{3,2,1,0:T(8,128)(2,1)}), bf16[4,3,64,512]{3,2,1,0:T(8,128)(2,1)}, u32[]{:S(2)}, u32[]{:S(2)}) %all-to-all-start.2) | async-done | bytes 786464 | tf_op jit(solution)/shard_map/all_to_all | solution.py:224
  313.7 4.2 all-to-all-start.3
  320.7 41.4 %shard_map.145 = (bf16[3,64,2048]{2,1,0:T(8,128)(2,1)S(1)}, bf16[3,64,2048]{2,1,0:T(8,128)(2,1)S(1)}, bf16[3,64,2048]{2,1,0:T(8,128)(2,1)S(1)}) custom-call(bf16[3,3,64,2048]{3,2,1,0:T(8,128)(2,1)S(1)} %copy-done.1, bf16[3,3,64,2048]{3,2,1,0:T(8,128)(2,1)S(1)} %copy-done.1, bf16[3,3,64,2048]{3,2,1,0:T(8,128)(2,1)S(1)} %copy-done.1, ...), custom_call_target="tpu_custom_call" | custom-call | flops 32212254720 | bytes 6291456 | tf_op jit(solution)/shard_map/pallas_call | solution.py:182
  365.0 41.2 %shard_map.146 = (bf16[3,64,2048]{2,1,0:T(8,128)(2,1)S(1)}, bf16[3,64,2048]{2,1,0:T(8,128)(2,1)S(1)}, bf16[3,64,2048]{2,1,0:T(8,128)(2,1)S(1)}) custom-call(bf16[3,3,64,2048]{3,2,1,0:T(8,128)(2,1)S(1)} %pad_maximum_fusion.2.q_ref.k_ref.v_ref, bf16[3,3,64,2048]{3,2,1,0:T(8,128)(2,1)S(1)} %pad_maximum_fusion.2.q_ref.k_ref.v_ref, ...), custom_call_target="tpu_custom_call" | custom-call | flops 32212254720 | bytes 6291456 | tf_op jit(solution)/shard_map/pallas_call | solution.py:182
  412.5 4.5 add_convert_fusion.4
  422.8 4.3 convolution_convert_fusion
  456.9 21.7 %all-gather.2 = bf16[384,576]{1,0:T(8,128)(2,1)S(1)} all-gather(bf16[96,576]{1,0:T(8,128)(2,1)} %reduce-scatter.13.cloned.1.call-done), channel_id=4, replica_groups=mesh['dp'=4,'ctx'=4,'fsdp'=2] {'ctx'}, dimensions={0}, use_global_device_ids=true | all-gather | bytes 552960 | tf_op jit(solution)/shard_map/all_gather | solution.py:337
  486.4 35.1 %reduce-scatter.7.cloned.1.call-done = bf16[512,768]{1,0:T(8,128)(2,1)} async-done(((bf16[2048,768]{1,0:T(8,128)(2,1)}), bf16[512,768]{1,0:T(8,128)(2,1)}) %reduce-scatter.7.cloned.1.call-update) | async-done | bytes 786448 | tf_op jit(solution)/shard_map/reduce_scatter | solution.py:326
  521.5 63.9 %reduce-scatter.9.cloned.1.call-done = bf16[512,768]{1,0:T(8,128)(2,1)} async-done(((bf16[2048,768]{1,0:T(8,128)(2,1)}), bf16[512,768]{1,0:T(8,128)(2,1)}) %reduce-scatter.9.cloned.1.call-update) | async-done | bytes 786448 | tf_op jit(solution)/shard_map/reduce_scatter | solution.py:326
  587.9 63.6 %reduce-scatter.11.cloned.1.call-done = bf16[1,528,768]{2,1,0:T(8,128)(2,1)} async-done(((bf16[8,528,768]{2,1,0:T(8,128)(2,1)}), bf16[1,528,768]{2,1,0:T(8,128)(2,1)}) %reduce-scatter.11.cloned.1.call-update) | async-done | bytes 811024 | tf_op jit(solution)/shard_map/reduce_scatter | solution.py:307
  656.1 42.3 %all-reduce.2.cloned.1.call-done = bf16[528,768]{1,0:T(8,128)(2,1)} async-done(((bf16[528,768]{1,0:T(8,128)(2,1)}), bf16[528,768]{1,0:T(8,128)(2,1)}) %all-reduce.2.cloned.1.call-update) | async-done | bytes 811024 | tf_op jit(solution)/shard_map/psum | solution.py:308
  (250 shorter events, 132.2 us)
Async XLA Ops:
  7.2 69.2 %all-gather.18.cloned.1.call-start = ((), (), s32[]{:S(2)}) async-start(), calls=%async_computation.16 | async-start | bytes 3932160 | tf_op jit(solution)/shard_map/all_gather | solution.py:253
  9.9 130.7 %all-gather.16.cloned.1.call-start = ((), (), s32[]{:S(2)}) async-start(), calls=%async_computation.15 | async-start | bytes 3932160 | tf_op jit(solution)/shard_map/all_gather | solution.py:253
  10.0 24.4 %copy-start.58 = (bf16[96]{0:T(256)(128)(2,1)S(1)}, bf16[96]{0:T(256)(128)(2,1)}, u32[]{:S(2)}) copy-start(bf16[96]{0:T(256)(128)(2,1)} %param.14) | copy-start | bytes 580
  10.0 24.4 %copy-start.60 = (bf16[96]{0:T(256)(128)(2,1)S(1)}, bf16[96]{0:T(256)(128)(2,1)}, u32[]{:S(2)}) copy-start(bf16[96]{0:T(256)(128)(2,1)} %param.15) | copy-start | bytes 580
  10.7 203.7 %all-gather.10.cloned.1.call-start = ((), (), s32[]{:S(2)}) async-start(), calls=%async_computation.8 | async-start | bytes 1327104 | tf_op jit(solution)/shard_map/all_gather | solution.py:220
  11.4 226.9 %all-gather.12.cloned.1.call-start = ((), (), s32[]{:S(2)}) async-start(), calls=%async_computation.9 | async-start | bytes 3981312 | tf_op jit(solution)/shard_map/all_gather | solution.py:220
  12.0 233.1 %all-gather.14.cloned.1.call-start = ((), (), s32[]{:S(2)}) async-start(), calls=%async_computation.10 | async-start | bytes 1990656 | tf_op jit(solution)/shard_map/all_gather | solution.py:220
  34.4 110.2 %copy-start.42 = (bf16[768,576]{1,0:T(8,128)(2,1)}, bf16[768,576]{1,0:T(8,128)(2,1)S(1)}, u32[]{:S(2)}) copy-start(bf16[768,576]{1,0:T(8,128)(2,1)S(1)} %all_gather.27) | copy-start | bytes 2654212
  47.9 96.6 %copy-start.44 = (f32[768]{0:T(1024)}, f32[768]{0:T(1024)S(1)}, u32[]{:S(2)}) copy-start(f32[768]{0:T(1024)S(1)} %get-tuple-element.41) | copy-start | bytes 9220
  176.6 32.7 %all-to-all-start.1 = ((bf16[4,3,64,512]{3,2,1,0:T(8,128)(2,1)}), bf16[4,3,64,512]{3,2,1,0:T(8,128)(2,1)}, u32[]{:S(2)}, u32[]{:S(2)}) async-start(bf16[4,3,64,512]{3,2,1,0:T(8,128)(2,1)} %copy-done.2), calls=%async_computation.1 | async-start | bytes 1572864 | tf_op jit(solution)/shard_map/all_to_all | solution.py:224
  209.3 24.8 %all-to-all-start = ((bf16[4,3,64,512]{3,2,1,0:T(8,128)(2,1)}), bf16[4,3,64,512]{3,2,1,0:T(8,128)(2,1)}, u32[]{:S(2)}, u32[]{:S(2)}) async-start(bf16[4,3,64,512]{3,2,1,0:T(8,128)(2,1)} %copy-done.4), calls=%async_computation | async-start | bytes 1572864 | tf_op jit(solution)/shard_map/all_to_all | solution.py:224
  245.0 19.3 %copy-start.29 = (f32[512,2304]{1,0:T(8,128)S(1)}, f32[512,2304]{1,0:T(8,128)}, u32[]{:S(2)}) copy-start(f32[512,2304]{1,0:T(8,128)} %fusion.82) | copy-start | bytes 14155780
  289.8 23.9 %all-to-all-start.2 = ((bf16[4,3,64,512]{3,2,1,0:T(8,128)(2,1)}), bf16[4,3,64,512]{3,2,1,0:T(8,128)(2,1)}, u32[]{:S(2)}, u32[]{:S(2)}) async-start(bf16[4,3,64,512]{3,2,1,0:T(8,128)(2,1)} %bitcast.184), calls=%async_computation.2 | async-start | bytes 1572864 | tf_op jit(solution)/shard_map/all_to_all | solution.py:224
  313.7 50.2 %all-to-all-start.3 = ((bf16[4,3,64,512]{3,2,1,0:T(8,128)(2,1)}), bf16[4,3,64,512]{3,2,1,0:T(8,128)(2,1)}, u32[]{:S(2)}, u32[]{:S(2)}) async-start(bf16[4,3,64,512]{3,2,1,0:T(8,128)(2,1)} %bitcast.183), calls=%async_computation.4 | async-start | bytes 1572864 | tf_op jit(solution)/shard_map/all_to_all | solution.py:224
  317.9 139.0 %reduce-scatter.13.cloned.1.call-start = ((), (), s32[]{:S(2)}) async-start(), calls=%async_computation.17 | async-start | bytes 1105920 | tf_op jit(solution)/shard_map/reduce_scatter | solution.py:334
  365.0 41.5 %copy-start.33 = (bf16[9,64,2048]{2,1,0:T(8,128)(2,1)S(1)}, bf16[9,64,2048]{2,1,0:T(8,128)(2,1)}, u32[]{:S(2)}) copy-start(bf16[9,64,2048]{2,1,0:T(8,128)(2,1)} %pad_maximum_fusion.4) | copy-start | bytes 7077892
  417.0 104.5 %reduce-scatter.7.cloned.1.call-start = ((), (), s32[]{:S(2)}) async-start(), calls=%async_computation.11 | async-start | bytes 3932160 | tf_op jit(solution)/shard_map/reduce_scatter | solution.py:326
  421.2 164.2 %reduce-scatter.9.cloned.1.call-start = ((), (), s32[]{:S(2)}) async-start(), calls=%async_computation.12 | async-start | bytes 3932160 | tf_op jit(solution)/shard_map/reduce_scatter | solution.py:326
  427.1 224.4 %reduce-scatter.11.cloned.1.call-start = ((), (), s32[]{:S(2)}) async-start(), calls=%async_computation.13 | async-start | bytes 7299072 | tf_op jit(solution)/shard_map/reduce_scatter | solution.py:307
  448.4 250.0 %all-reduce.2.cloned.1.call-start = ((), (), s32[]{:S(2)}) async-start(), calls=%async_computation.14 | async-start | bytes 1622016 | tf_op jit(solution)/shard_map/psum | solution.py:308
  479.5 6.4 copy-start.59
  484.3 167.2 %copy-start.12 = (f32[512,768]{1,0:T(8,128)S(1)}, f32[512,768]{1,0:T(8,128)}, u32[]{:S(2)}) copy-start(f32[512,768]{1,0:T(8,128)} %copy-done.10) | copy-start | bytes 4718596
  656.1 44.3 %copy-start.37 = (bf16[96,2304]{1,0:T(8,128)(2,1)S(1)}, bf16[96,2304]{1,0:T(8,128)(2,1)}, u32[]{:S(2)}) copy-start(bf16[96,2304]{1,0:T(8,128)(2,1)} %param.12) | copy-start | bytes 1327108
  656.1 45.4 %copy-start.61 = (bf16[96]{0:T(256)(128)(2,1)S(1)}, bf16[96]{0:T(256)(128)(2,1)}, u32[]{:S(2)}) copy-start(bf16[96]{0:T(256)(128)(2,1)} %param.15) | copy-start | bytes 580
  (56 other events, 150.7 us)
Sparse Core Ops, SparseCore 0:
  10.1 66.1 all-gather.17
  78.5 62.0 all-gather.15
  142.5 22.5 all-gather.9
  166.8 33.8 all-gather.11
  202.4 26.3 all-gather.13
  417.1 36.9 reduce-scatter.12
  457.0 64.4 reduce-scatter.6
  523.8 61.5 reduce-scatter.8
  588.9 62.6 reduce-scatter.10
  653.7 44.6 all-reduce.1
